TPU v7x, 256 devices: a whole 4x4x8 slice. The times are simulated.
256 devices in a mesh: rows: 256 (over y, z, x, core).
Axes of the slice: x: 4, y: 4, z: 8, core: 2. Of those that a mesh axis runs over, the one named last changes fastest.
Arguments:
- embeddings: bfloat16 [524288, 128], P('rows'), may hold values from -24 to 24
- labels: int32 [524288], P('rows'), may hold values from 0 to 64
- predictions: float32 [64, 524288], P(None, 'rows'), may hold values from -25 to 25
- coefficients: float32 [64, 524288], P(None, 'rows'), may hold values from -4 to 4
- block_index: int32 [2, 1024], replicated, may hold values from 0 to 2047, as said below
- owner_id: int32 [2], replicated, may hold values from 0 to 255
Outputs:
- new_predictions: float32 [64, 524288], P(None, 'rows')
- new_coefficients: float32 [64, 524288], P(None, 'rows')
- residual_norms: float32 [2, 64], replicated
Inputs may be any that keep to these rules, and one draw needn't show every extreme that they name: `block_index`: within each step the 1024 entries are distinct local rows of the owner; 0 and 2047 appear in every step.
All inputs are finite; a program needn't handle non-finite values.
Results may differ from a plain program's by a relative error of at most 0.008.
Values may be sent and summed in bfloat16 or wider, within the bound.
A program may use at most 128 MiB of HBM per device.

v0:
```python
import math

import jax
import jax.numpy as jnp
from jax import lax
from jax.sharding import PartitionSpec as P

RIDGE = 1.0


def spread(shard, axis, root):
    mine = lax.axis_index(axis) == root
    return lax.psum(jnp.where(mine, shard, jnp.zeros_like(shard)), axis)


def squares_of(points):
    widened = points.astype(jnp.float32)
    return jnp.sum(widened * widened, axis=1)


def kernel_tile(left_points, left_norms, right_points, right_norms):
    cross_term = lax.dot_general(
        left_points, right_points, (((1,), (1,)), ((), ())), preferred_element_type=jnp.float32
    )
    distance = left_norms[:, None] + right_norms[None, :] - 2.0 * cross_term
    return jnp.exp(distance * (-0.5 / left_points.shape[1]))


def solve_block(gram_matrix, right_side):
    factor = jnp.linalg.cholesky(gram_matrix)
    middle = lax.linalg.triangular_solve(
        factor, right_side, left_side=False, lower=True, transpose_a=True
    )
    return lax.linalg.triangular_solve(
        factor, middle, left_side=False, lower=True, transpose_a=False
    )


def local(embeddings, labels, predictions, coefficients, block_index, owner_id):
    rows_dev = embeddings.shape[0]
    device_index = lax.axis_index("rows")
    total_rows = rows_dev * lax.axis_size("rows")
    thresholds = jnp.arange(predictions.shape[0], dtype=jnp.int32)
    targets = (labels[None, :] <= thresholds[:, None]).astype(jnp.float32)
    row_norms = squares_of(embeddings)
    tile_rows = math.gcd(rows_dev, 1024)
    slab_points = embeddings.reshape(rows_dev // tile_rows, tile_rows, embeddings.shape[1])
    slab_norms = row_norms.reshape(rows_dev // tile_rows, tile_rows)
    eye_block = jnp.eye(block_index.shape[1], dtype=jnp.float32)
    new_predictions = predictions
    new_coefficients = coefficients
    residual = targets - new_predictions - RIDGE * new_coefficients
    norm_list = []
    for iteration in range(block_index.shape[0]):
        picked = block_index[iteration]
        is_owner = device_index == owner_id[iteration]
        owned_points = jnp.take(embeddings, picked, axis=0)
        owned_residual = jnp.take(residual, picked, axis=1)
        block_points = spread(owned_points, "rows", owner_id[iteration])
        block_norms = squares_of(block_points)

        def solve_here(right_side):
            gram_matrix = (
                kernel_tile(block_points, block_norms, block_points, block_norms)
                + RIDGE * eye_block
            )
            return solve_block(gram_matrix, right_side)

        local_update = lax.cond(is_owner, solve_here, jnp.zeros_like, owned_residual)
        update_half = spread(local_update.astype(jnp.bfloat16), "rows", owner_id[iteration])
        new_coefficients = new_coefficients.at[:, picked].add(local_update)

        def add_slab(pieces):
            kernel_block = kernel_tile(block_points, block_norms, pieces[0], pieces[1]).astype(
                jnp.bfloat16
            )
            return jnp.dot(update_half, kernel_block, preferred_element_type=jnp.float32)

        increment = lax.map(add_slab, (slab_points, slab_norms))
        new_predictions = new_predictions + jnp.transpose(increment, (1, 0, 2)).reshape(
            new_predictions.shape
        )
        residual = targets - new_predictions - RIDGE * new_coefficients
        partial_sum = jnp.sum(residual * residual, axis=1)
        totals = lax.psum(partial_sum, "rows")
        norm_list.append(jnp.sqrt(totals / total_rows + 1e-06))
    residual_norms = jnp.stack(norm_list)
    return (new_predictions, new_coefficients, residual_norms)


def solution(mesh):
    in_specs = (P("rows", None), P("rows"), P(None, "rows"), P(None, "rows"), P(), P())
    out_specs = (P(None, "rows"), P(None, "rows"), P())
    return jax.shard_map(local, mesh=mesh, in_specs=in_specs, out_specs=out_specs, check_vma=False)
```

profile of v0, /device:TPU:1, one launch (start us, length us, event | category | flops | bytes accessed | tf_op | source)
XLA Modules:
  0.0 1594.2 jit_solution(10906980618261843693)
XLA Ops:
  8.0 1.4 fusion.228
  10.1 4.0 gather_fusion
  19.6 4.0 gather_fusion.1
  25.4 3.2 gather_fusion.2
  29.5 2.4 fusion.216
  32.0 240.0 %all-reduce.7.cloned.1.call-done = bf16[1024,128]{1,0:T(8,128)(2,1)} async-done(((bf16[1024,128]{1,0:T(8,128)(2,1)}), bf16[1024,128]{1,0:T(8,128)(2,1)}) %all-reduce.7.cloned.1.call-update) | async-done | bytes 262160 | tf_op jit(solution)/shard_map/psum | solution.py:13
  271.9 1.7 multiply_reduce_fusion.3
  273.7 5.7 conditional.2
  282.7 6.4 scatter_fusion
  289.1 594.4 %all-reduce.11.cloned.1.call-done = (bf16[1024,128]{1,0:T(8,128)(2,1)}, bf16[64,1024]{1,0:T(8,128)(2,1)}) async-done(((bf16[1024,128]{1,0:T(8,128)(2,1)}, bf16[64,1024]{1,0:T(8,128)(2,1)}), (bf16[1024,128]{1,0:T(8,128)(2,1)}, bf16[64,1024]{1,0:T(8,128)(2,1)})) %all-reduce.11.cloned.1.call-update) | async-done | bytes 393232 | tf_op jit(solution)/shard_map/psum | solution.py:13
  883.6 4.6 while.30
  883.6 2.3 fusion.298
  885.9 2.3 fusion.298
  889.6 2.8 multiply_reduce_fusion
  892.4 4.0 gather_fusion.3
  898.3 4.9 conditional.3
  905.0 6.5 scatter_fusion.1
  912.7 587.3 %all-reduce.9.cloned.1.call-done = bf16[64,1024]{1,0:T(8,128)(2,1)} async-done(((bf16[64,1024]{1,0:T(8,128)(2,1)}), bf16[64,1024]{1,0:T(8,128)(2,1)}) %all-reduce.9.cloned.1.call-update) | async-done | bytes 131088 | tf_op jit(solution)/shard_map/psum | solution.py:13
  1500.0 4.6 while.31
  1500.1 2.3 fusion.302
  1502.4 2.3 fusion.302
  1506.0 2.5 fusion.221
  1508.5 2.3 copy.39
  1510.8 76.1 %all-reduce.1 = (f32[64]{0:T(128)S(1)}, f32[64]{0:T(128)S(1)}) all-reduce(f32[64]{0:T(128)S(1)} %get-tuple-element.224, f32[64]{0:T(128)S(1)} %copy-done.11), channel_id=1, replica_groups=mesh['rows'=256] {'rows'}, use_global_device_ids=true, to_apply=%region_36.42 | all-reduce | flops 128 | bytes 1024 | tf_op jit(solution)/shard_map/psum | solution.py:85
  (61 shorter events, 21.1 us)
Async XLA Ops:
  7.2 10.7 copy-start.5
  7.2 11.1 copy-start.6
  7.2 264.7 %all-reduce.7.cloned.1.call-start = ((), (), s32[]{:S(2)}) async-start(), calls=%async_computation | async-start | bytes 524288 | tf_op jit(solution)/shard_map/psum | solution.py:13
  15.0 868.5 %all-reduce.11.cloned.1.call-start = ((), (), s32[]{:S(2)}) async-start(), calls=%async_computation.2 | async-start | bytes 786432 | tf_op jit(solution)/shard_map/psum | solution.py:13
  15.1 10.2 copy-start.7
  15.1 13.5 copy-start.9
  17.9 7.4 copy-start
  279.4 604.2 %copy-start.4 = (bf16[1024,128]{1,0:T(8,128)(2,1)S(1)}, bf16[1024,128]{1,0:T(8,128)(2,1)}, u32[]{:S(2)}) copy-start(bf16[1024,128]{1,0:T(8,128)(2,1)} %all-reduce.7.cloned.1.call-done) | copy-start | bytes 786436
  280.1 1219.9 %all-reduce.9.cloned.1.call-start = ((), (), s32[]{:S(2)}) async-start(), calls=%async_computation.1 | async-start | bytes 262144 | tf_op jit(solution)/shard_map/psum | solution.py:13
  888.2 4.2 copy-start.8
  888.2 8.3 copy-start.10
  889.6 7.9 copy-start.3
  1504.6 6.2 copy-start.11
Sparse Core Ops, SparseCore 0:
  15.2 256.7 all-reduce.6
  280.2 603.2 all-reduce.10
  904.0 595.9 all-reduce.8
where the time goes:
time: 1600 us; the launch traced here: 1590 us
  waiting for transfers between devices  1420 us (89%)
  blocking collectives  76.1 us (5%)
  other arithmetic  33.2 us (2%)
  local copies, waits for them, and re-layouts  29.2 us (2%)
    psum x3, waiting for transfers between devices, spread(): return lax.psum(jnp.where(mine, shard, jnp.zeros_like(shard)), axis)  1420 us
    psum x1, blocking collectives, local(): totals = lax.psum(partial_sum, 'rows')  76.1 us
  transfers between devices with their start and end apart: 3, of which 3 were waited for; matrix products, arithmetic and copies ran while one was open for 2% of the time, Pallas kernels for 0%

commit v1 on v0

v1 whole, which is shorter than its diff:
```python
import functools

import jax
import jax.numpy as jnp
from jax import lax
from jax.experimental import pallas as pl
from jax.experimental.pallas import tpu as pltpu
from jax.sharding import PartitionSpec as P

F32, BF16, I32 = jnp.float32, jnp.bfloat16, jnp.int32
MESH = pl.DeviceIdType.MESH
NN = (((1,), (0,)), ((), ()))
NT = (((1,), (1,)), ((), ()))
TN = (((0,), (0,)), ((), ()))

RIDGE = 1.0
FEATURES = 128
TARGETS = 64
BLOCK = 1024
ROWS = 2048
NX, NY, NZ = 4, 4, 8
STRIDE_X, STRIDE_Z, STRIDE_Y = 2, 2 * NX, 2 * NX * NZ
PAY = 2048
NB = 256
STAGES = 7
VMEM_LIMIT = 60 << 20


def mm(a, b, dims=NN):
    return lax.dot_general(a, b, dims, preferred_element_type=F32)


def split(a):
    high = a.astype(BF16)
    return high, (a - high.astype(F32)).astype(BF16)


def mm3(a, b, dims=NN):
    return mm(a[0], b[0], dims) + (mm(a[0], b[1], dims) + mm(a[1], b[0], dims))


def iota(shape, dim):
    return lax.broadcasted_iota(I32, shape, dim)


def vmem():
    return pl.BlockSpec(memory_space=pltpu.VMEM)


def smem():
    return pl.BlockSpec(memory_space=pltpu.SMEM)


def residual_of(labels, predictions, coefficients):
    targets = (labels <= iota((TARGETS, labels.shape[1]), 0)).astype(F32)
    return targets - predictions - RIDGE * coefficients


def square_norms(points):
    wide = points.astype(F32)
    squares = wide * wide
    high, low = split(squares)
    ones = jnp.ones((8, points.shape[1]), BF16)
    row = (mm(ones, high, NT) + mm(ones, low, NT))[:1]
    return row, jnp.sum(squares, axis=1, keepdims=True)


def kernel_of(cross, left, right):
    return jnp.exp((left + right - 2.0 * cross) * (-0.5 / FEATURES))


def selection(picked, start, size):
    return (iota((size, picked.shape[1]), 0) + start == picked).astype(BF16)


def prep_kernel(owner_ref, points_ref, labels_ref, pred_ref, coef_ref, index_ref, out_ref):
    me = lax.axis_index("rows")
    for step in range(2):

        @pl.when(owner_ref[step] == me)
        def _():
            residual = residual_of(labels_ref[...], pred_ref[...], coef_ref[...])
            high, low = split(residual)
            picked = index_ref[step : step + 1, :]
            acc = jnp.zeros((256, BLOCK), F32)
            for start in range(0, ROWS, 256):
                rows = slice(start, start + 256)
                left = jnp.concatenate(
                    [points_ref[rows, :].T, high[:, rows], low[:, rows]], axis=0
                )
                acc = acc + mm(left, selection(picked, start, 256))
            for b in range(8):
                out_ref[step, b * 256 : (b + 1) * 256, :] = acc[:, b * 128 : (b + 1) * 128].astype(BF16)


def coords():
    me = lax.axis_index("rows")
    core = lax.rem(me, 2)
    x = lax.rem(lax.div(me, STRIDE_X), NX)
    z = lax.rem(lax.div(me, STRIDE_Z), NZ)
    y = lax.div(me, STRIDE_Y)
    return me, core, x, y, z


def peers(me, at, size, stride):
    out = []
    for hop in [d for k in range(1, size // 2 + 1) for d in ((k, -k) if 2 * k < size else (k,))]:
        position = lax.rem(at + hop + size, size)
        out.append((position, me + (position - at) * stride))
    return out


def spread_kernel(owner_ref, own_ref, out_ref, cand_c, cand_x, cand_y, cand_z, mine, send_sem, recv_sem):
    me, core, x, y, z = coords()
    other = me + 1 - 2 * core
    rings = ((peers(me, x, NX, STRIDE_X), x), (peers(me, y, NY, STRIDE_Y), y), (peers(me, z, NZ, STRIDE_Z), z))
    barrier = pltpu.get_barrier_semaphore()
    count = 1
    pl.semaphore_signal(barrier, inc=1, device_id=(other,), device_id_type=MESH)
    for ring, _ in rings:
        for _, device in ring:
            pl.semaphore_signal(barrier, inc=1, device_id=(device,), device_id_type=MESH)
            count += 1
    pl.semaphore_wait(barrier, count)

    owner = owner_ref[core]
    owner_at = (
        lax.rem(lax.div(owner, STRIDE_X), NX),
        lax.div(owner, STRIDE_Y),
        lax.rem(lax.div(owner, STRIDE_Z), NZ),
    )

    copy = pltpu.make_async_remote_copy(
        own_ref.at[1 - core], cand_c.at[core], send_sem.at[0, 0], recv_sem.at[0, 0],
        device_id=(other,), device_id_type=MESH,
    )
    copy.start()
    cand_c[core] = own_ref[core]
    copy.wait()

    held = cand_c
    held_at = lax.rem(owner, 2)
    size = PAY
    stages = (cand_x, cand_y, cand_z)
    for phase, (cand, (ring, at)) in enumerate(zip(stages, rings), 1):
        members = cand.shape[0]
        mine[0:size, :] = held[held_at]
        piece = size // members
        copies = []
        for position, device in ring:
            copy = pltpu.make_async_remote_copy(
                mine.at[pl.ds(pl.multiple_of(position * piece, piece), piece), :],
                cand.at[at], send_sem.at[phase, position], recv_sem.at[phase, at],
                device_id=(device,), device_id_type=MESH,
            )
            copy.start()
            copies.append(copy)
        cand[at] = mine[pl.ds(pl.multiple_of(at * piece, piece), piece), :]
        for copy in copies:
            copy.wait_send()
        for position, device in ring:
            pltpu.make_async_remote_copy(
                cand.at[position], cand.at[position], send_sem.at[phase, position],
                recv_sem.at[phase, position], device_id=(device,), device_id_type=MESH,
            ).wait_recv()
        held, held_at, size = cand, owner_at[phase - 1], piece

    start = x * (PAY // NX) + y * (PAY // NX // NY) + z * size
    out_ref[pl.ds(pl.multiple_of(start, size), size), :] = held[held_at]
    for phase, (ring, at), members in ((4, rings[2], NZ), (5, rings[1], NY), (6, rings[0], NX)):
        here = pl.ds(pl.multiple_of(start, size), size)
        base = start - at * size
        copies = []
        for position, device in ring:
            copy = pltpu.make_async_remote_copy(
                out_ref.at[here, :], out_ref.at[here, :], send_sem.at[phase, position],
                recv_sem.at[phase, at], device_id=(device,), device_id_type=MESH,
            )
            copy.start()
            copies.append(copy)
        for copy in copies:
            copy.wait_send()
        for position, device in ring:
            there = pl.ds(pl.multiple_of(base + position * size, size), size)
            pltpu.make_async_remote_copy(
                out_ref.at[there, :], out_ref.at[there, :], send_sem.at[phase, position],
                recv_sem.at[phase, position], device_id=(device,), device_id_type=MESH,
            ).wait_recv()
        start, size = base, size * members


def unpack_points(pay_ref):
    return jnp.concatenate([pay_ref[b * 256 : b * 256 + 128, :].T for b in range(8)], axis=0)


def unpack_residual(pay_ref, part):
    lo = 128 + 64 * part
    return jnp.concatenate([pay_ref[b * 256 + lo : b * 256 + lo + 64, :] for b in range(8)], axis=1)


def inverse(matrix):
    n = matrix.shape[0]
    eye = (iota((n, n), 0) == iota((n, n), 1)).astype(F32)
    top = jnp.max(jnp.sum(jnp.abs(matrix), axis=0, keepdims=True), axis=1, keepdims=True)
    gain = 2.0 / (1.0 + top)
    rest = eye - gain * matrix
    scale = (top + 1.0) / jnp.maximum(top - 1.0, 1e-2)
    c = 1.0 + 1.0 / (2.0 * scale * scale - 1.0)
    result = (c * gain) * (eye + rest)
    parts = split(rest)
    for _ in range(STAGES - 1):
        rest = c * mm3(parts, parts) - (c - 1.0) * eye
        scale = jnp.minimum(2.0 * scale * scale - 1.0, 1e4)
        c = 1.0 + 1.0 / (2.0 * scale * scale - 1.0)
        parts = split(rest)
        result = c * (result + mm3(split(result), parts))
    return result


def block(k):
    return slice(k * NB, (k + 1) * NB)


def forward(k, v_ref, u_ref, xh_ref, xl_ref, wh_ref, wl_ref):
    v = split(v_ref[:, block(k)])
    if (k + 1) * NB < BLOCK:
        rest = slice((k + 1) * NB, BLOCK)
        v_ref[:, rest] = v_ref[:, rest] - mm3(v, (wh_ref[block(k), rest], wl_ref[block(k), rest]))
    u_ref[:, block(k)] = mm3(v, (xh_ref[k], xl_ref[k]))


def backward(u_ref, wh_ref, wl_ref):
    for j in range(BLOCK // NB - 1, 0, -1):
        u = split(u_ref[:, block(j)])
        for k in range(j):
            w = (wh_ref[block(k), block(j)], wl_ref[block(k), block(j)])
            u_ref[:, block(k)] = u_ref[:, block(k)] - mm3(u, w, NT)


def solve_kernel(pay_ref, points_ref, u_ref, xh_ref, xl_ref, wh_ref, wl_ref, g_ref, v_ref, uf_ref):
    points_ref[...] = unpack_points(pay_ref)
    norm_row, norm_col = square_norms(points_ref[...])
    count = BLOCK // NB
    for i in range(count):
        cross = mm(points_ref[block(i), :], points_ref[i * NB :, :], NT)
        tile = kernel_of(cross, norm_col[block(i)], norm_row[:, i * NB :])
        diagonal = (iota(tile.shape, 0) == iota(tile.shape, 1)).astype(F32)
        g_ref[block(i), i * NB :] = tile + RIDGE * diagonal
    v_ref[...] = unpack_residual(pay_ref, 0).astype(F32) + unpack_residual(pay_ref, 1).astype(F32)
    for k in range(count):
        x = split(inverse(g_ref[block(k), block(k)]))
        xh_ref[k], xl_ref[k] = x
        if k + 1 < count:
            rest = slice((k + 1) * NB, BLOCK)
            g = split(g_ref[block(k), rest])
            w = split(mm3(x, g))
            wh_ref[block(k), rest], wl_ref[block(k), rest] = w
            for i in range(k + 1, count):
                lo = (i - k - 1) * NB
                gi = (g[0][:, lo : lo + NB], g[1][:, lo : lo + NB])
                wi = (w[0][:, lo:], w[1][:, lo:])
                g_ref[block(i), i * NB :] = g_ref[block(i), i * NB :] - mm3(gi, wi, TN)
        forward(k, v_ref, uf_ref, xh_ref, xl_ref, wh_ref, wl_ref)
    backward(uf_ref, wh_ref, wl_ref)
    high, low = split(uf_ref[...])
    u_ref[0:TARGETS, :] = high
    u_ref[TARGETS:, :] = low


def swap_kernel(*refs):
    count = (len(refs) - 2) // 2
    sources, targets = refs[:count], refs[count : 2 * count]
    send_sem, recv_sem = refs[2 * count :]
    me = lax.axis_index("rows")
    other = me + 1 - 2 * lax.rem(me, 2)
    barrier = pltpu.get_barrier_semaphore()
    pl.semaphore_signal(barrier, inc=1, device_id=(other,), device_id_type=MESH)
    pl.semaphore_wait(barrier, 1)
    copies = []
    for i in range(count):
        copy = pltpu.make_async_remote_copy(
            sources[i], targets[i], send_sem.at[i], recv_sem.at[i],
            device_id=(other,), device_id_type=MESH,
        )
        copy.start()
        copies.append(copy)
    for copy in copies:
        copy.wait()


def swap(arrays, collective_id):
    return pl.pallas_call(
        swap_kernel,
        out_shape=[jax.ShapeDtypeStruct(a.shape, a.dtype) for a in arrays],
        in_specs=[vmem()] * len(arrays),
        out_specs=[vmem()] * len(arrays),
        scratch_shapes=[pltpu.SemaphoreType.DMA((len(arrays),)), pltpu.SemaphoreType.DMA((len(arrays),))],
        compiler_params=pltpu.CompilerParams(collective_id=collective_id, has_side_effects=True),
        name="swap",
    )(*arrays)


def second_kernel(
    owner_ref, pay_ref, mine_ref, first_ref, u1_ref, index_ref, xh_ref, xl_ref, wh_ref, wl_ref,
    u_ref, v_ref, uf_ref,
):
    core = lax.rem(lax.axis_index("rows"), 2)

    @pl.when(core == 1)
    def _():
        right, _ = square_norms(mine_ref[...])
        _, left = square_norms(first_ref[...])
        v = unpack_residual(pay_ref, 0).astype(F32) + unpack_residual(pay_ref, 1).astype(F32)
        for i in range(0, BLOCK, 256):
            rows = slice(i, i + 256)
            cross = mm(first_ref[rows, :], mine_ref[...], NT)
            half = kernel_of(cross, left[rows], right).astype(BF16)
            v = v - mm(u1_ref[0:TARGETS, rows], half)
        v_ref[...] = v

    @pl.when((core == 1) & (owner_ref[0] == owner_ref[1]))
    def _():
        placed = place(u1_ref[...], index_ref[0:1, :]).astype(BF16)
        both = jnp.zeros((2 * TARGETS, BLOCK), F32)
        for start in range(0, ROWS, 256):
            both = both + mm(placed[:, start : start + 256], selection(index_ref[1:2, :], start, 256))
        v_ref[...] = v_ref[...] - RIDGE * (both[:TARGETS] + both[TARGETS:])

    @pl.when(core == 1)
    def _():
        for k in range(BLOCK // NB):
            forward(k, v_ref, uf_ref, xh_ref, xl_ref, wh_ref, wl_ref)
        backward(uf_ref, wh_ref, wl_ref)
        high, low = split(uf_ref[...])
        u_ref[0:TARGETS, :] = high
        u_ref[TARGETS:, :] = low


def place(update, picked):
    return jnp.concatenate(
        [mm(update, selection(picked, start, 256), NT) for start in range(0, ROWS, 256)], axis=1
    )


def apply_kernel(
    owner_ref, rows_ref, labels_ref, pred_ref, coef_ref, index_ref, pm_ref, po_ref, um_ref, uo_ref, vo_ref,
    new_pred_ref, new_coef_ref, sums_ref, block_ref, half_ref,
):
    me = lax.axis_index("rows")
    core = lax.rem(me, 2)

    @pl.when(core == 0)
    def _():
        block_ref[0] = pm_ref[...]
        block_ref[1] = po_ref[...]
        half_ref[0] = um_ref[...]
        half_ref[1] = vo_ref[...]

    @pl.when(core == 1)
    def _():
        block_ref[0] = po_ref[...]
        block_ref[1] = pm_ref[...]
        half_ref[0] = uo_ref[...]
        half_ref[1] = um_ref[...]

    right, _ = square_norms(rows_ref[...])
    new_coef_ref[...] = coef_ref[...]
    columns = []
    for step in range(2):

        @pl.when(owner_ref[step] == me)
        def _():
            both = place(half_ref[step], index_ref[step : step + 1, :])
            new_coef_ref[...] = new_coef_ref[...] + (both[:TARGETS] + both[TARGETS:])

        _, left = square_norms(block_ref[step])
        before = pred_ref if step == 0 else new_pred_ref
        total = jnp.zeros((TARGETS, 1), F32)
        for start in range(0, ROWS, 256):
            cols = slice(start, start + 256)
            cross = mm(block_ref[step], rows_ref[cols, :], NT)
            half = kernel_of(cross, left, right[:, cols]).astype(BF16)
            new = before[:, cols] + mm(half_ref[step, 0:TARGETS, :], half)
            new_pred_ref[:, cols] = new
            residual = residual_of(labels_ref[:, cols], new, new_coef_ref[:, cols])
            total = total + jnp.sum(residual * residual, axis=1, keepdims=True)
        columns.append(total)
    sums = jnp.broadcast_to(jnp.concatenate(columns, axis=0), (128, 128))
    sums_ref[...] = sums.T[0:8, :]


def norm_kernel(total_rows, sums_ref, out_ref, got_a, got_y, got_z, send_sem, recv_sem):
    me, core, x, y, z = coords()
    here = core + 2 * x
    plane = []
    for hop in range(1, 2 * NX):
        position = lax.rem(here + hop, 2 * NX)
        plane.append((position, me + position - here))
    rings = (
        (plane, here, got_a),
        (peers(me, y, NY, STRIDE_Y), y, got_y),
        (peers(me, z, NZ, STRIDE_Z), z, got_z),
    )
    barrier = pltpu.get_barrier_semaphore()
    count = 0
    for ring, _, _ in rings:
        for _, device in ring:
            pl.semaphore_signal(barrier, inc=1, device_id=(device,), device_id_type=MESH)
            count += 1
    pl.semaphore_wait(barrier, count)
    value = sums_ref[...]
    for phase, (ring, at, got) in enumerate(rings):
        got[at] = value
        copies = []
        for position, device in ring:
            copy = pltpu.make_async_remote_copy(
                got.at[at], got.at[at], send_sem.at[phase, position], recv_sem.at[phase, at],
                device_id=(device,), device_id_type=MESH,
            )
            copy.start()
            copies.append(copy)
        for copy in copies:
            copy.wait_send()
        for position, device in ring:
            pltpu.make_async_remote_copy(
                got.at[position], got.at[position], send_sem.at[phase, position],
                recv_sem.at[phase, position], device_id=(device,), device_id_type=MESH,
            ).wait_recv()
        value = jnp.sum(got[...], axis=0)
    norms = jnp.sqrt(value / total_rows + 1e-06)
    out_ref[0:1, :] = norms[0:1, 0:TARGETS]
    out_ref[1:2, :] = norms[0:1, TARGETS:]


def local(embeddings, labels, predictions, coefficients, block_index, owner_id):
    shape = jax.ShapeDtypeStruct
    total_rows = embeddings.shape[0] * lax.axis_size("rows")
    labels = labels.reshape(1, ROWS)
    params = pltpu.CompilerParams(vmem_limit_bytes=VMEM_LIMIT)

    own = pl.pallas_call(
        prep_kernel,
        out_shape=shape((2, PAY, 128), BF16),
        in_specs=[smem()] + [vmem()] * 5,
        out_specs=vmem(),
        compiler_params=params,
        name="prep",
    )(owner_id, embeddings, labels, predictions, coefficients, block_index)

    pay = pl.pallas_call(
        spread_kernel,
        out_shape=shape((PAY, 128), BF16),
        in_specs=[smem(), vmem()],
        out_specs=vmem(),
        scratch_shapes=[
            pltpu.VMEM((2, PAY, 128), BF16),
            pltpu.VMEM((NX, PAY // NX, 128), BF16),
            pltpu.VMEM((NY, PAY // NX // NY, 128), BF16),
            pltpu.VMEM((NZ, PAY // NX // NY // NZ, 128), BF16),
            pltpu.VMEM((PAY, 128), BF16),
            pltpu.SemaphoreType.DMA((7, 8)),
            pltpu.SemaphoreType.DMA((7, 8)),
        ],
        compiler_params=pltpu.CompilerParams(
            collective_id=0, has_side_effects=True, vmem_limit_bytes=VMEM_LIMIT
        ),
        name="spread",
    )(owner_id, own)

    count = BLOCK // NB
    points, update, xh, xl, wh, wl = pl.pallas_call(
        solve_kernel,
        out_shape=[
            shape((BLOCK, FEATURES), BF16),
            shape((2 * TARGETS, BLOCK), BF16),
            shape((count, NB, NB), BF16),
            shape((count, NB, NB), BF16),
            shape((BLOCK, BLOCK), BF16),
            shape((BLOCK, BLOCK), BF16),
        ],
        in_specs=[vmem()],
        out_specs=[vmem()] * 6,
        scratch_shapes=[
            pltpu.VMEM((BLOCK, BLOCK), F32),
            pltpu.VMEM((TARGETS, BLOCK), F32),
            pltpu.VMEM((TARGETS, BLOCK), F32),
        ],
        compiler_params=params,
        name="solve",
    )(pay)

    other_points, other_update = swap([points, update], 1)

    second = pl.pallas_call(
        second_kernel,
        out_shape=shape((2 * TARGETS, BLOCK), BF16),
        in_specs=[smem()] + [vmem()] * 9,
        out_specs=vmem(),
        scratch_shapes=[pltpu.VMEM((TARGETS, BLOCK), F32), pltpu.VMEM((TARGETS, BLOCK), F32)],
        compiler_params=params,
        name="second",
    )(owner_id, pay, points, other_points, other_update, block_index, xh, xl, wh, wl)

    (other_second,) = swap([second], 2)
    core = lax.rem(lax.axis_index("rows"), 2)
    mine = jnp.where(core == 0, update, second)

    new_pred, new_coef, sums = pl.pallas_call(
        apply_kernel,
        out_shape=[
            shape((TARGETS, ROWS), F32),
            shape((TARGETS, ROWS), F32),
            shape((8, 128), F32),
        ],
        in_specs=[smem()] + [vmem()] * 10,
        out_specs=[vmem()] * 3,
        scratch_shapes=[
            pltpu.VMEM((2, BLOCK, FEATURES), BF16),
            pltpu.VMEM((2, 2 * TARGETS, BLOCK), BF16),
        ],
        compiler_params=params,
        name="apply",
    )(
        owner_id, embeddings, labels, predictions, coefficients, block_index,
        points, other_points, mine, other_update, other_second,
    )

    norms = pl.pallas_call(
        functools.partial(norm_kernel, total_rows),
        out_shape=shape((2, TARGETS), F32),
        in_specs=[vmem()],
        out_specs=vmem(),
        scratch_shapes=[
            pltpu.VMEM((2 * NX, 8, 128), F32),
            pltpu.VMEM((NY, 8, 128), F32),
            pltpu.VMEM((NZ, 8, 128), F32),
            pltpu.SemaphoreType.DMA((3, 8)),
            pltpu.SemaphoreType.DMA((3, 8)),
        ],
        compiler_params=pltpu.CompilerParams(collective_id=3, has_side_effects=True),
        name="norms",
    )(sums)
    return new_pred, new_coef, norms


def solution(mesh):
    in_specs = (P("rows", None), P("rows"), P(None, "rows"), P(None, "rows"), P(), P())
    out_specs = (P(None, "rows"), P(None, "rows"), P())
    return jax.shard_map(local, mesh=mesh, in_specs=in_specs, out_specs=out_specs, check_vma=False)
```

time: 1600 us -> 111 us (0.07)
  waiting for transfers between devices: 1420 us -> 0 us
  Pallas kernels: 0 us -> 107 us
  blocking collectives: 76.1 us -> 0 us
  other arithmetic: 33.2 us -> 1.71 us
  local copies, waits for them, and re-layouts: 29.2 us -> 1.2 us
    psum x3 -> x0, waiting for transfers between devices: 1420 us -> none  [spread(): return lax.psum(jnp.where(mine, shard, jnp.zeros_like(shard)), axis)]
    pallas_call x0 -> x8, Pallas kernels: none -> 107 us  [the longest x1 42.4 us: local(): pl.pallas_call(spread_kernel, out_shape=shape((PAY, 128), BF16), in_specs...]
    psum x1 -> x0, blocking collectives: 76.1 us -> none  [local(): totals = lax.psum(partial_sum, 'rows')]
  transfers between devices with their start and end apart: 3 -> 0, of which waited for: 3 -> 0; matrix products, arithmetic and copies ran while one was open for 2% -> 0% of each run, Pallas kernels for 0% -> 0%
where the time goes in v1:
time: 111 us
  Pallas kernels  107 us (96%)
  other arithmetic  1.71 us (2%)
  local copies, waits for them, and re-layouts  1.2 us (1%)
    pallas_call x1, Pallas kernels, local(): pl.pallas_call(spread_kernel, out_shape=shape((PAY, 128), BF16), in_specs...  42.4 us
    pallas_call x1, Pallas kernels, local(): pl.pallas_call(solve_kernel, out_shape=[shape((BLOCK, FEATURES), BF16), s...  16.8 us
    pallas_call x1, Pallas kernels, local(): pl.pallas_call(functools.partial(norm_kernel, total_rows), out_shape=shap...  15.9 us
    pallas_call x2, Pallas kernels, swap(): pl.pallas_call(swap_kernel, out_shape=[jax.ShapeDtypeStruct(a.shape, a.dt...  11.2 us
    pallas_call x1, Pallas kernels, local(): pl.pallas_call(apply_kernel, out_shape=[shape((TARGETS, ROWS), F32), shap...  10.8 us
    pallas_call x1, Pallas kernels, local(): pl.pallas_call(second_kernel, out_shape=shape((2 * TARGETS, BLOCK), BF16)...  7.93 us
    pallas_call x1, Pallas kernels, local(): pl.pallas_call(prep_kernel, out_shape=shape((2, PAY, 128), BF16), in_spec...  2.38 us

profile of v1, /device:TPU:1, one launch (start us, length us, event | category | flops | bytes accessed | tf_op | source)
XLA Modules:
  0.0 110.9 jit_solution(16394744579587341663)
XLA Ops:
  0.6 2.4 %prep.1.own_ref = bf16[2,2048,128]{2,1,0:T(8,128)(2,1)} custom-call(s32[2]{0:T(128)} %owner_ref.7, bf16[2048,128]{1,0:T(8,128)(2,1)} %rows_ref.1, s32[1,2048]{1,0:T(1,128)} %bitcast.1, f32[64,2048]{1,0:T(8,128)} %pred_ref.3, f32[64,2048]{1,0:T(8,128)} %coef_ref.3, s32[2,1024]{1,0:T(2,128)} %index_ref.5), custom_call_target="tpu_custom_call" | custom-call | tf_op jit(solution)/shard_map/prep/pallas_call | solution.py:441
  3.0 42.4 %spread.1.pay_ref = bf16[2048,128]{1,0:T(8,128)(2,1)} custom-call(s32[2]{0:T(128)} %owner_ref.7, bf16[2,2048,128]{2,1,0:T(8,128)(2,1)} %prep.1.own_ref), custom_call_target="tpu_custom_call" | custom-call | tf_op jit(solution)/shard_map/spread/pallas_call | solution.py:450
  45.4 16.8 %solve.1 = (bf16[1024,128]{1,0:T(8,128)(2,1)}, bf16[128,1024]{1,0:T(8,128)(2,1)}, bf16[4,256,256]{2,1,0:T(8,128)(2,1)}, bf16[4,256,256]{2,1,0:T(8,128)(2,1)}, bf...) custom-call(bf16[2048,128]{1,0:T(8,128)(2,1)} %spread.1.pay_ref), custom_call_target="tpu_custom_call" | custom-call | tf_op jit(solution)/shard_map/solve/pallas_call | solution.py:471
  62.1 8.0 %swap.2 = (bf16[1024,128]{1,0:T(8,128)(2,1)}, bf16[128,1024]{1,0:T(8,128)(2,1)}) custom-call(bf16[1024,128]{1,0:T(8,128)(2,1)} %get-tuple-element.14.refs_0_.mine_ref.pm_ref, bf16[128,1024]{1,0:T(8,128)(2,1)} %get-tuple-element.15.refs_1_), custom_call_target="tpu_custom_call" | custom-call | tf_op jit(solution)/shard_map/swap/pallas_call | solution.py:292
  70.2 0.0 copy-start
  70.2 7.9 %second.1.refs_0_ = bf16[128,1024]{1,0:T(8,128)(2,1)} custom-call(s32[2]{0:T(128)} %owner_ref.7, bf16[2048,128]{1,0:T(8,128)(2,1)} %spread.1.pay_ref, bf16[1024,128]{1,0:T(8,128)(2,1)} %get-tuple-element.14.refs_0_.mine_ref.pm_ref, bf16[1024,128]{1,0:T(8,128)(2,1)} %get-tuple-element.16.first_ref.po_ref, bf16[128,1024]{1,0:T(8,128)(2,1)} %get-tuple-element.17.u1_ref.uo_ref, ...), custom_call_target="tpu_custom_call" | custom-call | tf_op jit(solution)/shard_map/second/pallas_call | solution.py:494
  78.1 0.0 copy-done
  78.1 1.7 %broadcast_select_fusion.um_ref = bf16[128,1024]{1,0:T(8,128)(2,1)} fusion(bf16[128,1024]{1,0:T(8,128)(2,1)S(1)} %copy-done, bf16[128,1024]{1,0:T(8,128)(2,1)} %second.1.refs_0_, pred[]{:T(512)S(6)} %eq.3), kind=kLoop, calls=%fused_computation | loop fusion | flops 131072 | bytes 786433 | tf_op jit(solution)/shard_map/jit(_where)/select_n | solution.py:506
  79.8 3.2 %swap.3.vo_ref = bf16[128,1024]{1,0:T(8,128)(2,1)} custom-call(bf16[128,1024]{1,0:T(8,128)(2,1)} %second.1.refs_0_), custom_call_target="tpu_custom_call" | custom-call | tf_op jit(solution)/shard_map/swap/pallas_call | solution.py:292
  83.0 10.8 %apply.1 = (f32[64,2048]{1,0:T(8,128)}, f32[64,2048]{1,0:T(8,128)}, f32[8,128]{1,0:T(8,128)}) custom-call(s32[2]{0:T(128)} %owner_ref.7, bf16[2048,128]{1,0:T(8,128)(2,1)} %rows_ref.1, s32[1,2048]{1,0:T(1,128)} %bitcast.2, f32[64,2048]{1,0:T(8,128)} %pred_ref.3, f32[64,2048]{1,0:T(8,128)} %coef_ref.3, s32[2,1024]{1,0:T(2,128)} %index_ref.5, ...), custom_call_target="tpu_custom_call" | custom-call | tf_op jit(solution)/shard_map/apply/pallas_call | solution.py:508
  93.8 15.9 %norms.1 = f32[2,64]{1,0:T(2,128)} custom-call(f32[8,128]{1,0:T(8,128)} %get-tuple-element.24.sums_ref), custom_call_target="tpu_custom_call" | custom-call | tf_op jit(solution)/shard_map/norms/pallas_call | solution.py:528
  109.7 1.2 %copy.10 = f32[2,64]{1,0:T(2,128)} copy(f32[2,64]{1,0:T(2,128)} %norms.1) | data formatting | bytes 1024
Async XLA Ops:
  70.2 7.9 %copy-start = (bf16[128,1024]{1,0:T(8,128)(2,1)S(1)}, bf16[128,1024]{1,0:T(8,128)(2,1)}, u32[]{:S(2)}) copy-start(bf16[128,1024]{1,0:T(8,128)(2,1)} %get-tuple-element.15.refs_1_) | copy-start | bytes 786436

commit v2 on v1

v2 whole, which is shorter than its diff:
```python
import functools

import jax
import jax.numpy as jnp
from jax import lax
from jax.experimental import pallas as pl
from jax.experimental.pallas import tpu as pltpu
from jax.sharding import PartitionSpec as P

F32, BF16, I32 = jnp.float32, jnp.bfloat16, jnp.int32
MESH = pl.DeviceIdType.MESH
NN = (((1,), (0,)), ((), ()))
NT = (((1,), (1,)), ((), ()))
TN = (((0,), (0,)), ((), ()))

RIDGE = 1.0
FEATURES = 128
TARGETS = 64
BLOCK = 1024
ROWS = 2048
NX, NY, NZ = 4, 4, 8
STRIDE_X, STRIDE_Z, STRIDE_Y = 2, 2 * NX, 2 * NX * NZ
NB = 256
STAGES = 7
VMEM_LIMIT = 60 << 20


def mm(a, b, dims=NN):
    return lax.dot_general(a, b, dims, preferred_element_type=F32)


def split(a):
    high = a.astype(BF16)
    return high, (a - high.astype(F32)).astype(BF16)


def mm3(a, b, dims=NN):
    return mm(a[0], b[0], dims) + (mm(a[0], b[1], dims) + mm(a[1], b[0], dims))


def iota(shape, dim):
    return lax.broadcasted_iota(I32, shape, dim)


def vmem():
    return pl.BlockSpec(memory_space=pltpu.VMEM)


def smem():
    return pl.BlockSpec(memory_space=pltpu.SMEM)


def residual_of(labels, predictions, coefficients):
    targets = (labels <= iota((TARGETS, labels.shape[1]), 0)).astype(F32)
    return targets - predictions - RIDGE * coefficients


def square_norms(points):
    wide = points.astype(F32)
    squares = wide * wide
    high, low = split(squares)
    ones = jnp.ones((8, points.shape[1]), BF16)
    row = (mm(ones, high, NT) + mm(ones, low, NT))[:1]
    return row, jnp.sum(squares, axis=1, keepdims=True)


def kernel_of(cross, left, right):
    return jnp.exp((left + right - 2.0 * cross) * (-0.5 / FEATURES))


def selection(picked, start, size):
    return (iota((size, picked.shape[1]), 0) + start == picked).astype(BF16)


def coords():
    me = lax.axis_index("rows")
    core = lax.rem(me, 2)
    x = lax.rem(lax.div(me, STRIDE_X), NX)
    z = lax.rem(lax.div(me, STRIDE_Z), NZ)
    y = lax.div(me, STRIDE_Y)
    return me, core, x, y, z


def hops(size):
    return sorted(range(size), key=lambda d: -min(d, size - d))


def ring_peers(me, at, size, stride):
    out = []
    for hop in hops(size):
        if hop:
            position = lax.rem(at + hop, size)
            out.append((position, me + (position - at) * stride))
    return out


def plane_peers(me, x, y):
    pairs = [(dx, dy) for dx in range(NX) for dy in range(NY) if dx or dy]
    pairs.sort(key=lambda d: -(min(d[0], NX - d[0]) + min(d[1], NY - d[1])))
    out = []
    for dx, dy in pairs:
        px, py = lax.rem(x + dx, NX), lax.rem(y + dy, NY)
        out.append((py * NX + px, me + (px - x) * STRIDE_X + (py - y) * STRIDE_Y))
    return out


def aligned(start, size):
    return pl.ds(pl.multiple_of(start, size), size)


class Broadcast:
    def __init__(self, plane, z_ring, places, owner_places, refs, sems):
        self.plane, self.z_ring = plane, z_ring
        self.at, self.z = places
        self.owner_at, self.owner_z = owner_places
        self.whole, self.cand_p, self.cand_z, self.out = refs
        self.send, self.recv = sems

    def run(self, phase, source, target, peers, at):
        copies = []
        for position, device in peers:
            copies.append(
                pltpu.make_async_remote_copy(
                    source(position), target(at), self.send.at[phase, position],
                    self.recv.at[phase, at], device_id=(device,), device_id_type=MESH,
                )
            )
            copies[-1].start()

        def wait():
            for copy in copies:
                copy.wait_send()
            for position, device in peers:
                pltpu.make_async_remote_copy(
                    target(position), target(position), self.send.at[phase, position],
                    self.recv.at[phase, position], device_id=(device,), device_id_type=MESH,
                ).wait_recv()

        return wait

    def scatter(self):
        piece = self.cand_p.shape[1]
        wait = self.run(
            0, lambda p: self.whole.at[aligned(p * piece, piece), :], lambda p: self.cand_p.at[p],
            self.plane, self.at,
        )
        self.cand_p[self.at] = self.whole[aligned(self.at * piece, piece), :]
        return wait

    def exchange(self):
        self.cand_z[self.z] = self.cand_p[self.owner_at]
        return self.run(
            1, lambda p: self.cand_z.at[self.z], lambda p: self.cand_z.at[p], self.z_ring, self.z
        )

    def gather(self):
        piece = self.cand_p.shape[1]
        target = lambda p: self.out.at[aligned(p * piece, piece), :]
        self.out[aligned(self.at * piece, piece), :] = self.cand_z[self.owner_z]
        return self.run(2, lambda p: target(self.at), target, self.plane, self.at)


def inverse(matrix):
    n = matrix.shape[0]
    eye = (iota((n, n), 0) == iota((n, n), 1)).astype(F32)
    top = jnp.max(jnp.sum(jnp.abs(matrix), axis=0, keepdims=True), axis=1, keepdims=True)
    gain = 2.0 / (1.0 + top)
    rest = eye - gain * matrix
    scale = (top + 1.0) / jnp.maximum(top - 1.0, 1e-2)
    c = 1.0 + 1.0 / (2.0 * scale * scale - 1.0)
    result = (c * gain) * (eye + rest)
    parts = split(rest)
    for _ in range(STAGES - 1):
        rest = c * mm3(parts, parts) - (c - 1.0) * eye
        scale = jnp.minimum(2.0 * scale * scale - 1.0, 1e4)
        c = 1.0 + 1.0 / (2.0 * scale * scale - 1.0)
        parts = split(rest)
        result = c * (result + mm3(split(result), parts))
    return result


def block(k):
    return slice(k * NB, (k + 1) * NB)


def forward(k, v_ref, u_ref, xh_ref, xl_ref, wh_ref, wl_ref):
    v = split(v_ref[:, block(k)])
    if (k + 1) * NB < BLOCK:
        rest = slice((k + 1) * NB, BLOCK)
        v_ref[:, rest] = v_ref[:, rest] - mm3(v, (wh_ref[block(k), rest], wl_ref[block(k), rest]))
    u_ref[:, block(k)] = mm3(v, (xh_ref[k], xl_ref[k]))


def backward(u_ref, wh_ref, wl_ref):
    for j in range(BLOCK // NB - 1, 0, -1):
        u = split(u_ref[:, block(j)])
        for k in range(j):
            w = (wh_ref[block(k), block(j)], wl_ref[block(k), block(j)])
            u_ref[:, block(k)] = u_ref[:, block(k)] - mm3(u, w, NT)


def factor(points_ref, norm_row, norm_col, g_ref, xh_ref, xl_ref, wh_ref, wl_ref, after):
    count = BLOCK // NB
    for i in range(count):
        cross = mm(points_ref[block(i), :], points_ref[i * NB :, :], NT)
        tile = kernel_of(cross, norm_col[block(i)], norm_row[:, i * NB :])
        diagonal = (iota(tile.shape, 0) == iota(tile.shape, 1)).astype(F32)
        g_ref[block(i), i * NB :] = tile + RIDGE * diagonal
    for k in range(count):
        xh_ref[k], xl_ref[k] = split(inverse(g_ref[block(k), block(k)]))
        x = xh_ref[k], xl_ref[k]
        if k + 1 < count:
            rest = slice((k + 1) * NB, BLOCK)
            g = split(g_ref[block(k), rest])
            w = split(mm3(x, g))
            wh_ref[block(k), rest], wl_ref[block(k), rest] = w
            for i in range(k + 1, count):
                lo = (i - k - 1) * NB
                gi = (g[0][:, lo : lo + NB], g[1][:, lo : lo + NB])
                wi = (w[0][:, lo:], w[1][:, lo:])
                g_ref[block(i), i * NB :] = g_ref[block(i), i * NB :] - mm3(gi, wi, TN)
        after(k)


def updates_kernel(
    owner_ref, rows_ref, labels_ref, pred_ref, coef_ref, index_ref, points_ref, u_ref,
    own, got, whole_p, whole_r, cand_pp, cand_pz, cand_rp, cand_rz, res_ref,
    pts_ref, g_ref, xh_ref, xl_ref, wh_ref, wl_ref, v_ref, uf_ref, k12_ref, same_ref,
    send_p, recv_p, send_r, recv_r, send_c, recv_c,
):
    me, core, x, y, z = coords()
    other = me + 1 - 2 * core
    plane = plane_peers(me, x, y)
    z_ring = ring_peers(me, z, NZ, STRIDE_Z)

    barrier = pltpu.get_barrier_semaphore()
    pl.semaphore_signal(barrier, inc=1, device_id=(other,), device_id_type=MESH)
    for _, device in plane + z_ring:
        pl.semaphore_signal(barrier, inc=1, device_id=(device,), device_id_type=MESH)

    def across(number, source, target):
        return pltpu.make_async_remote_copy(
            source, target, send_c.at[number], recv_c.at[number],
            device_id=(other,), device_id_type=MESH,
        )

    high, low = split(residual_of(labels_ref[...], pred_ref[...], coef_ref[...]))
    left = jnp.concatenate([rows_ref[...].T, high, low], axis=0)

    def prepare(step):
        picked = index_ref[pl.ds(step, 1), :]
        acc = jnp.zeros((256, BLOCK), F32)
        for start in range(0, ROWS, 256):
            acc = acc + mm(left[:, start : start + 256], selection(picked, start, 256))
        acc = acc.astype(BF16)
        for b in range(8):
            own[0, b * 128 : (b + 1) * 128, :] = acc[:128, b * 128 : (b + 1) * 128]
            own[1, b * 128 : (b + 1) * 128, :] = acc[128:, b * 128 : (b + 1) * 128]

    owner = owner_ref[core]
    owner_core = lax.rem(owner, 2)
    owner_at = lax.div(owner, STRIDE_Y) * NX + lax.rem(lax.div(owner, STRIDE_X), NX)
    owner_z = lax.rem(lax.div(owner, STRIDE_Z), NZ)

    prepare(1 - core)
    pl.semaphore_wait(barrier, 1 + len(plane) + len(z_ring))
    send_points = across(0, own.at[0], got.at[0])
    send_points.start()
    send_residual = across(1, own.at[1], got.at[1])
    send_residual.start()
    send_points.wait()
    send_residual.wait()
    prepare(core)

    places, owner_places = (y * NX + x, z), (owner_at, owner_z)
    points = Broadcast(
        plane, z_ring, places, owner_places, (whole_p, cand_pp, cand_pz, pts_ref), (send_p, recv_p)
    )
    residual = Broadcast(
        plane, z_ring, places, owner_places, (whole_r, cand_rp, cand_rz, res_ref), (send_r, recv_r)
    )
    mine = owner_core == core
    whole_p[...] = jnp.where(mine, own[0], got[0])
    wait_p = points.scatter()
    whole_r[...] = jnp.where(mine, own[1], got[1])
    wait_p()
    wait_p = points.exchange()
    wait_r = residual.scatter()
    wait_p()
    wait_p = points.gather()
    wait_r()
    wait_r = residual.exchange()
    wait_p()
    for b in range(8):
        points_ref[core, b * 128 : (b + 1) * 128, :] = pts_ref[b * 128 : (b + 1) * 128, :].T
    share = across(2, points_ref.at[core], points_ref.at[core])
    share.start()
    wait_r()
    wait_r = residual.gather()

    my_points = points_ref.at[core]
    norm_row, norm_col = square_norms(my_points[...])

    def load_residual():
        part = lambda lo: jnp.concatenate(
            [res_ref[b * 128 + lo : b * 128 + lo + 64, :] for b in range(8)], axis=1
        )
        return part(0).astype(F32) + part(64).astype(F32)

    def after(k):
        if k == 0:
            wait_r()
            v_ref[...] = load_residual()
        forward(k, v_ref, uf_ref, xh_ref, xl_ref, wh_ref, wl_ref)

    factor(my_points, norm_row, norm_col, g_ref, xh_ref, xl_ref, wh_ref, wl_ref, after)
    share.wait()

    @pl.when(core == 0)
    def _():
        backward(uf_ref, wh_ref, wl_ref)
        u_ref[0, 0:TARGETS, :], u_ref[0, TARGETS:, :] = split(uf_ref[...])
        send = across(3, u_ref.at[0], u_ref.at[0])
        send.start()
        send.wait_send()
        across(4, u_ref.at[1], u_ref.at[1]).wait_recv()

    @pl.when(core == 1)
    def _():
        both = owner_ref[0] == owner_ref[1]
        _, left_col = square_norms(points_ref[0])
        first = index_ref[0:1, :].astype(F32)
        for i in range(0, BLOCK, 128):
            rows = slice(i, i + 128)
            cross = mm(points_ref[0, rows, :], points_ref[1], NT)
            column = jnp.broadcast_to(first[:, rows], (128, 128)).T[:, 0:1].astype(I32)
            same = ((column == index_ref[1:2, :]) & both).astype(BF16)
            same_ref[rows, :] = same
            k12_ref[rows, :] = kernel_of(cross, left_col[rows], norm_row).astype(BF16) + same
        v_ref[...] = load_residual()
        across(3, u_ref.at[0], u_ref.at[0]).wait_recv()
        v_ref[...] = v_ref[...] - (
            mm(u_ref[0, 0:TARGETS, :], k12_ref[...]) + mm(u_ref[0, TARGETS:, :], same_ref[...])
        )
        for k in range(BLOCK // NB):
            forward(k, v_ref, uf_ref, xh_ref, xl_ref, wh_ref, wl_ref)
        backward(uf_ref, wh_ref, wl_ref)
        u_ref[1, 0:TARGETS, :], u_ref[1, TARGETS:, :] = split(uf_ref[...])
        send = across(4, u_ref.at[1], u_ref.at[1])
        send.start()
        send.wait_send()


def place(update, picked):
    return jnp.concatenate(
        [mm(update, selection(picked, start, 256), NT) for start in range(0, ROWS, 256)], axis=1
    )


def apply_kernel(
    owner_ref, rows_ref, labels_ref, pred_ref, coef_ref, index_ref, block_ref, half_ref,
    new_pred_ref, new_coef_ref, sums_ref,
):
    me = lax.axis_index("rows")
    right, _ = square_norms(rows_ref[...])
    new_coef_ref[...] = coef_ref[...]
    columns = []
    for step in range(2):

        @pl.when(owner_ref[step] == me)
        def _():
            both = place(half_ref[step], index_ref[step : step + 1, :])
            new_coef_ref[...] = new_coef_ref[...] + (both[:TARGETS] + both[TARGETS:])

        _, left = square_norms(block_ref[step])
        before = pred_ref if step == 0 else new_pred_ref
        total = jnp.zeros((TARGETS, 1), F32)
        for start in range(0, ROWS, 256):
            cols = slice(start, start + 256)
            cross = mm(block_ref[step], rows_ref[cols, :], NT)
            half = kernel_of(cross, left, right[:, cols]).astype(BF16)
            new = before[:, cols] + mm(half_ref[step, 0:TARGETS, :], half)
            new_pred_ref[:, cols] = new
            residual = residual_of(labels_ref[:, cols], new, new_coef_ref[:, cols])
            total = total + jnp.sum(residual * residual, axis=1, keepdims=True)
        columns.append(total)
    sums = jnp.broadcast_to(jnp.concatenate(columns, axis=0), (128, 128))
    sums_ref[...] = sums.T[0:8, :]


def norm_kernel(total_rows, sums_ref, out_ref, got_a, got_y, got_z, send_sem, recv_sem):
    me, core, x, y, z = coords()
    here = core + 2 * x
    plane = []
    for hop in range(1, 2 * NX):
        position = lax.rem(here + hop, 2 * NX)
        plane.append((position, me + position - here))
    rings = (
        (plane, here, got_a),
        (ring_peers(me, y, NY, STRIDE_Y), y, got_y),
        (ring_peers(me, z, NZ, STRIDE_Z), z, got_z),
    )
    barrier = pltpu.get_barrier_semaphore()
    count = 0
    for ring, _, _ in rings:
        for _, device in ring:
            pl.semaphore_signal(barrier, inc=1, device_id=(device,), device_id_type=MESH)
            count += 1
    pl.semaphore_wait(barrier, count)
    value = sums_ref[...]
    for phase, (ring, at, got) in enumerate(rings):
        got[at] = value
        copies = []
        for position, device in ring:
            copy = pltpu.make_async_remote_copy(
                got.at[at], got.at[at], send_sem.at[phase, position], recv_sem.at[phase, at],
                device_id=(device,), device_id_type=MESH,
            )
            copy.start()
            copies.append(copy)
        for copy in copies:
            copy.wait_send()
        for position, device in ring:
            pltpu.make_async_remote_copy(
                got.at[position], got.at[position], send_sem.at[phase, position],
                recv_sem.at[phase, position], device_id=(device,), device_id_type=MESH,
            ).wait_recv()
        value = jnp.sum(got[...], axis=0)
    norms = jnp.sqrt(value / total_rows + 1e-06)
    out_ref[0:1, :] = norms[0:1, 0:TARGETS]
    out_ref[1:2, :] = norms[0:1, TARGETS:]


def local(embeddings, labels, predictions, coefficients, block_index, owner_id):
    shape = jax.ShapeDtypeStruct
    total_rows = embeddings.shape[0] * lax.axis_size("rows")
    labels = labels.reshape(1, ROWS)
    params = pltpu.CompilerParams(vmem_limit_bytes=VMEM_LIMIT)

    count = BLOCK // NB
    half = (BLOCK, 128)
    points, update = pl.pallas_call(
        updates_kernel,
        out_shape=[shape((2, BLOCK, FEATURES), BF16), shape((2, 2 * TARGETS, BLOCK), BF16)],
        in_specs=[smem()] + [vmem()] * 5,
        out_specs=[vmem()] * 2,
        scratch_shapes=[
            pltpu.VMEM((2,) + half, BF16),
            pltpu.VMEM((2,) + half, BF16),
            pltpu.VMEM(half, BF16),
            pltpu.VMEM(half, BF16),
            pltpu.VMEM((NX * NY, BLOCK // NX // NY, 128), BF16),
            pltpu.VMEM((NZ, BLOCK // NX // NY, 128), BF16),
            pltpu.VMEM((NX * NY, BLOCK // NX // NY, 128), BF16),
            pltpu.VMEM((NZ, BLOCK // NX // NY, 128), BF16),
            pltpu.VMEM(half, BF16),
            pltpu.VMEM(half, BF16),
            pltpu.VMEM((BLOCK, BLOCK), F32),
            pltpu.VMEM((count, NB, NB), BF16),
            pltpu.VMEM((count, NB, NB), BF16),
            pltpu.VMEM((BLOCK, BLOCK), BF16),
            pltpu.VMEM((BLOCK, BLOCK), BF16),
            pltpu.VMEM((TARGETS, BLOCK), F32),
            pltpu.VMEM((TARGETS, BLOCK), F32),
            pltpu.VMEM((BLOCK, BLOCK), BF16),
            pltpu.VMEM((BLOCK, BLOCK), BF16),
        ]
        + [pltpu.SemaphoreType.DMA((3, NX * NY))] * 4
        + [pltpu.SemaphoreType.DMA((5,))] * 2,
        compiler_params=pltpu.CompilerParams(
            collective_id=0, has_side_effects=True, vmem_limit_bytes=VMEM_LIMIT
        ),
        name="updates",
    )(owner_id, embeddings, labels, predictions, coefficients, block_index)

    new_pred, new_coef, sums = pl.pallas_call(
        apply_kernel,
        out_shape=[
            shape((TARGETS, ROWS), F32),
            shape((TARGETS, ROWS), F32),
            shape((8, 128), F32),
        ],
        in_specs=[smem()] + [vmem()] * 7,
        out_specs=[vmem()] * 3,
        compiler_params=params,
        name="apply",
    )(owner_id, embeddings, labels, predictions, coefficients, block_index, points, update)

    norms = pl.pallas_call(
        functools.partial(norm_kernel, total_rows),
        out_shape=shape((2, TARGETS), F32),
        in_specs=[vmem()],
        out_specs=vmem(),
        scratch_shapes=[
            pltpu.VMEM((2 * NX, 8, 128), F32),
            pltpu.VMEM((NY, 8, 128), F32),
            pltpu.VMEM((NZ, 8, 128), F32),
            pltpu.SemaphoreType.DMA((3, 8)),
            pltpu.SemaphoreType.DMA((3, 8)),
        ],
        compiler_params=pltpu.CompilerParams(collective_id=1, has_side_effects=True),
        name="norms",
    )(sums)
    return new_pred, new_coef, norms


def solution(mesh):
    in_specs = (P("rows", None), P("rows"), P(None, "rows"), P(None, "rows"), P(), P())
    out_specs = (P(None, "rows"), P(None, "rows"), P())
    return jax.shard_map(local, mesh=mesh, in_specs=in_specs, out_specs=out_specs, check_vma=False)
```

time: 111 us -> 83.1 us (0.75)
  Pallas kernels: 107 us -> 81 us
  other arithmetic: 1.71 us -> 0 us
    pallas_call x6 -> x1, Pallas kernels: 80.6 us -> 56 us  [local(): pl.pallas_call(updates_kernel, out_shape=[shape((2, BLOCK, FEATURES), BF1...]
    select_n x1 -> x0, other arithmetic: 1.71 us -> none  [local(): mine = jnp.where(core == 0, update, second)]
    pallas_call x1, Pallas kernels: 15.9 us -> 14.4 us  [local(): pl.pallas_call(functools.partial(norm_kernel, total_rows), out_shape=shap...]
where the time goes in v2:
time: 83.1 us; the launch traced here: 82.9 us
  Pallas kernels  81 us (97%)
  local copies, waits for them, and re-layouts  1.22 us (1%)
    pallas_call x1, Pallas kernels, local(): pl.pallas_call(updates_kernel, out_shape=[shape((2, BLOCK, FEATURES), BF1...  56 us
    pallas_call x1, Pallas kernels, local(): pl.pallas_call(functools.partial(norm_kernel, total_rows), out_shape=shap...  14.4 us
    pallas_call x1, Pallas kernels, local(): pl.pallas_call(apply_kernel, out_shape=[shape((TARGETS, ROWS), F32), shap...  10.6 us

profile of v2, /device:TPU:1, one launch (start us, length us, event | category | flops | bytes accessed | tf_op | source)
XLA Modules:
  0.0 82.9 jit_solution(208775658704490507)
XLA Ops:
  0.6 56.0 %updates.1 = (bf16[2,1024,128]{2,1,0:T(8,128)(2,1)}, bf16[2,128,1024]{2,1,0:T(8,128)(2,1)}) custom-call(s32[2]{0:T(128)} %owner_ref.3, bf16[2048,128]{1,0:T(8,128)(2,1)} %rows_ref.3, s32[1,2048]{1,0:T(1,128)} %bitcast.1, f32[64,2048]{1,0:T(8,128)} %pred_ref.3, f32[64,2048]{1,0:T(8,128)} %coef_ref.3, s32[2,1024]{1,0:T(2,128)} %index_ref.3), custom_call_target="tpu_custom_call" | custom-call | tf_op jit(solution)/shard_map/updates/pallas_call | solution.py:442
  56.7 10.6 %apply.1 = (f32[64,2048]{1,0:T(8,128)}, f32[64,2048]{1,0:T(8,128)}, f32[8,128]{1,0:T(8,128)}) custom-call(s32[2]{0:T(128)} %owner_ref.3, bf16[2048,128]{1,0:T(8,128)(2,1)} %rows_ref.3, s32[1,2048]{1,0:T(1,128)} %bitcast.2, f32[64,2048]{1,0:T(8,128)} %pred_ref.3, f32[64,2048]{1,0:T(8,128)} %coef_ref.3, s32[2,1024]{1,0:T(2,128)} %index_ref.3, ...), custom_call_target="tpu_custom_call" | custom-call | tf_op jit(solution)/shard_map/apply/pallas_call | solution.py:476
  67.3 14.4 %norms.1 = f32[2,64]{1,0:T(2,128)} custom-call(f32[8,128]{1,0:T(8,128)} %get-tuple-element.12.sums_ref), custom_call_target="tpu_custom_call" | custom-call | tf_op jit(solution)/shard_map/norms/pallas_call | solution.py:489
  81.7 1.2 %copy.10 = f32[2,64]{1,0:T(2,128)} copy(f32[2,64]{1,0:T(2,128)} %norms.1) | data formatting | bytes 1024

commit v3 on v2

v3 whole, which is shorter than its diff:
```python
import functools

import jax
import jax.numpy as jnp
from jax import lax
from jax.experimental import pallas as pl
from jax.experimental.pallas import tpu as pltpu
from jax.sharding import PartitionSpec as P

F32, BF16, I32 = jnp.float32, jnp.bfloat16, jnp.int32
MESH = pl.DeviceIdType.MESH
NN = (((1,), (0,)), ((), ()))
NT = (((1,), (1,)), ((), ()))
TN = (((0,), (0,)), ((), ()))

RIDGE = 1.0
LOG2E = 1.4426950408889634
FEATURES = 128
TARGETS = 64
BLOCK = 1024
ROWS = 2048
NX, NY, NZ = 4, 4, 8
STRIDE_X, STRIDE_Z, STRIDE_Y = 2, 2 * NX, 2 * NX * NZ
NB = 256
STAGES = 7
VMEM_LIMIT = 60 << 20


def mm(a, b, dims=NN):
    return lax.dot_general(a, b, dims, preferred_element_type=F32)


def split(a):
    high = a.astype(BF16)
    return high, (a - high.astype(F32)).astype(BF16)


def mm3(a, b, dims=NN):
    return mm(a[0], b[0], dims) + (mm(a[0], b[1], dims) + mm(a[1], b[0], dims))


def iota(shape, dim):
    return lax.broadcasted_iota(I32, shape, dim)


def vmem():
    return pl.BlockSpec(memory_space=pltpu.VMEM)


def smem():
    return pl.BlockSpec(memory_space=pltpu.SMEM)


def residual_of(labels, predictions, coefficients):
    targets = (labels <= iota((TARGETS, labels.shape[1]), 0)).astype(F32)
    return targets - predictions - RIDGE * coefficients


def augment(points):
    wide = points.astype(F32)
    high, low = split(wide * wide)
    ones = jnp.full((FEATURES, FEATURES), 0.5, BF16)
    half = mm(high, ones) + mm(low, ones)
    first, rest = half.astype(BF16), half
    rest = rest - first.astype(F32)
    second = rest.astype(BF16)
    third = (rest - second.astype(F32)).astype(BF16)
    lane = iota(half.shape, 1)
    parts = lambda at: jnp.where(
        lane == at, first.astype(F32),
        jnp.where(lane == at + 1, second.astype(F32),
                  jnp.where(lane == at + 2, third.astype(F32), 0.0)),
    )
    unit = lambda at: ((lane >= at) & (lane < at + 3)).astype(F32)
    left = (parts(0) + unit(3)).astype(BF16)
    right = (-unit(0) - parts(3)).astype(BF16)
    return jnp.concatenate([points, left], axis=1), jnp.concatenate([points, right], axis=1)


def kernel_of(left, right):
    return jnp.exp2(mm(left, right, NT) * (LOG2E / FEATURES))


def selection(picked, start, size):
    return (iota((size, picked.shape[1]), 0) + start == picked).astype(BF16)


def coords():
    me = lax.axis_index("rows")
    core = lax.rem(me, 2)
    x = lax.rem(lax.div(me, STRIDE_X), NX)
    z = lax.rem(lax.div(me, STRIDE_Z), NZ)
    y = lax.div(me, STRIDE_Y)
    return me, core, x, y, z


def hops(size):
    return sorted(range(size), key=lambda d: -min(d, size - d))


def ring_peers(me, at, size, stride):
    out = []
    for hop in hops(size):
        if hop:
            position = lax.rem(at + hop, size)
            out.append((position, me + (position - at) * stride))
    return out


def plane_peers(me, x, y):
    pairs = [(dx, dy) for dx in range(NX) for dy in range(NY) if dx or dy]
    pairs.sort(key=lambda d: -(min(d[0], NX - d[0]) + min(d[1], NY - d[1])))
    out = []
    for dx, dy in pairs:
        px, py = lax.rem(x + dx, NX), lax.rem(y + dy, NY)
        out.append((py * NX + px, me + (px - x) * STRIDE_X + (py - y) * STRIDE_Y))
    return out


def aligned(start, size):
    return pl.ds(pl.multiple_of(start, size), size)


class Broadcast:
    def __init__(self, plane, z_ring, places, owner_places, refs, sems):
        self.plane, self.z_ring = plane, z_ring
        self.at, self.z = places
        self.owner_at, self.owner_z = owner_places
        self.whole, self.cand_p, self.cand_z, self.out = refs
        self.send, self.recv = sems

    def run(self, phase, source, target, peers, at):
        copies = []
        for position, device in peers:
            copies.append(
                pltpu.make_async_remote_copy(
                    source(position), target(at), self.send.at[phase, position],
                    self.recv.at[phase, at], device_id=(device,), device_id_type=MESH,
                )
            )
            copies[-1].start()

        def wait():
            for copy in copies:
                copy.wait_send()
            for position, device in peers:
                pltpu.make_async_remote_copy(
                    target(position), target(position), self.send.at[phase, position],
                    self.recv.at[phase, position], device_id=(device,), device_id_type=MESH,
                ).wait_recv()

        return wait

    def scatter(self):
        piece = self.cand_p.shape[1]
        wait = self.run(
            0, lambda p: self.whole.at[aligned(p * piece, piece), :], lambda p: self.cand_p.at[p],
            self.plane, self.at,
        )
        self.cand_p[self.at] = self.whole[aligned(self.at * piece, piece), :]
        return wait

    def exchange(self):
        self.cand_z[self.z] = self.cand_p[self.owner_at]
        return self.run(
            1, lambda p: self.cand_z.at[self.z], lambda p: self.cand_z.at[p], self.z_ring, self.z
        )

    def gather(self):
        piece = self.cand_p.shape[1]
        target = lambda p: self.out.at[aligned(p * piece, piece), :]
        self.out[aligned(self.at * piece, piece), :] = self.cand_z[self.owner_z]
        return self.run(2, lambda p: target(self.at), target, self.plane, self.at)


def inverse(matrix):
    n = matrix.shape[0]
    eye = (iota((n, n), 0) == iota((n, n), 1)).astype(F32)
    top = jnp.max(jnp.sum(jnp.abs(matrix), axis=0, keepdims=True), axis=1, keepdims=True)
    gain = 2.0 / (1.0 + top)
    rest = eye - gain * matrix
    scale = (top + 1.0) / jnp.maximum(top - 1.0, 1e-2)
    c = 1.0 + 1.0 / (2.0 * scale * scale - 1.0)
    result = (c * gain) * (eye + rest)
    parts = split(rest)
    for _ in range(STAGES - 1):
        rest = c * mm3(parts, parts) - (c - 1.0) * eye
        scale = jnp.minimum(2.0 * scale * scale - 1.0, 1e4)
        c = 1.0 + 1.0 / (2.0 * scale * scale - 1.0)
        parts = split(rest)
        result = c * (result + mm3(split(result), parts))
    return result


def block(k):
    return slice(k * NB, (k + 1) * NB)


def forward(k, v_ref, u_ref, xh_ref, xl_ref, wh_ref, wl_ref):
    v = split(v_ref[:, block(k)])
    if (k + 1) * NB < BLOCK:
        rest = slice((k + 1) * NB, BLOCK)
        v_ref[:, rest] = v_ref[:, rest] - mm3(v, (wh_ref[block(k), rest], wl_ref[block(k), rest]))
    u_ref[:, block(k)] = mm3(v, (xh_ref[k], xl_ref[k]))


def backward(u_ref, wh_ref, wl_ref):
    for j in range(BLOCK // NB - 1, 0, -1):
        u = split(u_ref[:, block(j)])
        for k in range(j):
            w = (wh_ref[block(k), block(j)], wl_ref[block(k), block(j)])
            u_ref[:, block(k)] = u_ref[:, block(k)] - mm3(u, w, NT)


def factor(left_ref, right_ref, g_ref, xh_ref, xl_ref, wh_ref, wl_ref, after):
    count = BLOCK // NB
    for i in range(count):
        tile = kernel_of(left_ref[block(i), :], right_ref[i * NB :, :])
        diagonal = (iota(tile.shape, 0) == iota(tile.shape, 1)).astype(F32)
        g_ref[block(i), i * NB :] = tile + RIDGE * diagonal
    for k in range(count):
        xh_ref[k], xl_ref[k] = split(inverse(g_ref[block(k), block(k)]))
        x = xh_ref[k], xl_ref[k]
        if k + 1 < count:
            rest = slice((k + 1) * NB, BLOCK)
            g = split(g_ref[block(k), rest])
            w = split(mm3(x, g))
            wh_ref[block(k), rest], wl_ref[block(k), rest] = w
            for i in range(k + 1, count):
                lo = (i - k - 1) * NB
                gi = (g[0][:, lo : lo + NB], g[1][:, lo : lo + NB])
                wi = (w[0][:, lo:], w[1][:, lo:])
                g_ref[block(i), i * NB :] = g_ref[block(i), i * NB :] - mm3(gi, wi, TN)
        after(k)


def descend_kernel(
    owner_ref, rows_ref, labels_ref, pred_ref, coef_ref, index_ref,
    new_pred_ref, new_coef_ref, sums_ref,
    own, got, whole_p, whole_r, cand_pp, cand_pz, cand_rp, cand_rz, pts_ref, res_ref,
    sel_ref, right_ref, points_ref, left_ref, mine_ref, u_ref,
    g_ref, xh_ref, xl_ref, wh_ref, wl_ref, v_ref, uf_ref, k12_ref, same_ref,
    got_c, got_p, got_z,
    send_p, recv_p, send_r, recv_r, send_n, recv_n, send_c, recv_c,
):
    me, core, x, y, z = coords()
    other = me + 1 - 2 * core
    plane = plane_peers(me, x, y)
    z_ring = ring_peers(me, z, NZ, STRIDE_Z)
    place_at = y * NX + x

    barrier = pltpu.get_barrier_semaphore()
    pl.semaphore_signal(barrier, inc=1, device_id=(other,), device_id_type=MESH)
    for _, device in plane + z_ring:
        pl.semaphore_signal(barrier, inc=1, device_id=(device,), device_id_type=MESH)

    def across(number, source, target):
        return pltpu.make_async_remote_copy(
            source, target, send_c.at[number], recv_c.at[number],
            device_id=(other,), device_id_type=MESH,
        )

    high, low = split(residual_of(labels_ref[...], pred_ref[...], coef_ref[...]))
    left = jnp.concatenate([rows_ref[...].T, high, low], axis=0)

    def prepare(slot, step):
        picked = index_ref[pl.ds(step, 1), :]
        acc = jnp.zeros((256, BLOCK), F32)
        for start in range(0, ROWS, 256):
            rows = slice(start, start + 256)
            chosen = selection(picked, start, 256)
            sel_ref[step, rows, :] = chosen
            acc = acc + mm(left[:, rows], chosen)
        acc = acc.astype(BF16)
        for b in range(8):
            own[slot, 0, b * 128 : (b + 1) * 128, :] = acc[:128, b * 128 : (b + 1) * 128]
            own[slot, 1, b * 128 : (b + 1) * 128, :] = acc[128:, b * 128 : (b + 1) * 128]

    owner = owner_ref[core]
    owner_core = lax.rem(owner, 2)
    owner_at = lax.div(owner, STRIDE_Y) * NX + lax.rem(lax.div(owner, STRIDE_X), NX)
    owner_z = lax.rem(lax.div(owner, STRIDE_Z), NZ)

    prepare(1, 1 - core)
    pl.semaphore_wait(barrier, 1 + len(plane) + len(z_ring))
    send_points = across(0, own.at[1, 0], got.at[0])
    send_points.start()
    send_residual = across(1, own.at[1, 1], got.at[1])
    send_residual.start()
    prepare(0, core)

    places, owner_places = (place_at, z), (owner_at, owner_z)
    points = Broadcast(
        plane, z_ring, places, owner_places, (whole_p, cand_pp, cand_pz, pts_ref), (send_p, recv_p)
    )
    residual = Broadcast(
        plane, z_ring, places, owner_places, (whole_r, cand_rp, cand_rz, res_ref), (send_r, recv_r)
    )
    mine = owner_core == core
    send_points.wait()
    whole_p[...] = jnp.where(mine, own[0, 0], got[0])
    wait_p = points.scatter()
    send_residual.wait()
    whole_r[...] = jnp.where(mine, own[0, 1], got[1])
    right_ref[...] = augment(rows_ref[...])[1]
    wait_p()
    wait_p = points.exchange()
    wait_r = residual.scatter()
    new_coef_ref[...] = coef_ref[...]
    wait_p()
    wait_p = points.gather()
    wait_r()
    wait_r = residual.exchange()
    wait_p()
    for b in range(8):
        points_ref[core, b * 128 : (b + 1) * 128, :] = pts_ref[b * 128 : (b + 1) * 128, :].T
    share = across(2, points_ref.at[core], points_ref.at[core])
    share.start()
    wait_r()
    wait_r = residual.gather()

    left_ref[core], mine_ref[...] = augment(points_ref[core])

    def load_residual():
        part = lambda lo: jnp.concatenate(
            [res_ref[b * 128 + lo : b * 128 + lo + 64, :] for b in range(8)], axis=1
        )
        return part(0).astype(F32) + part(64).astype(F32)

    def after(k):
        if k == 0:
            wait_r()
            v_ref[...] = load_residual()
        forward(k, v_ref, uf_ref, xh_ref, xl_ref, wh_ref, wl_ref)

    factor(left_ref.at[core], mine_ref, g_ref, xh_ref, xl_ref, wh_ref, wl_ref, after)
    share.wait()

    @pl.when(core == 0)
    def _():
        backward(uf_ref, wh_ref, wl_ref)
        u_ref[0, 0:TARGETS, :], u_ref[0, TARGETS:, :] = split(uf_ref[...])
        across(3, u_ref.at[0], u_ref.at[0]).start()

    left_ref[1 - core] = augment(points_ref[1 - core])[0]

    @pl.when(core == 1)
    def _():
        both = owner_ref[0] == owner_ref[1]
        first = index_ref[0:1, :].astype(F32)
        for i in range(0, BLOCK, 128):
            rows = slice(i, i + 128)
            column = jnp.broadcast_to(first[:, rows], (128, 128)).T[:, 0:1].astype(I32)
            same = ((column == index_ref[1:2, :]) & both).astype(BF16)
            same_ref[rows, :] = same
            k12_ref[rows, :] = kernel_of(left_ref[0, rows, :], mine_ref[...]).astype(BF16) + same
        v_ref[...] = load_residual()
        across(3, u_ref.at[0], u_ref.at[0]).wait_recv()
        v_ref[...] = v_ref[...] - (
            mm(u_ref[0, 0:TARGETS, :], k12_ref[...]) + mm(u_ref[0, TARGETS:, :], same_ref[...])
        )
        for k in range(BLOCK // NB):
            forward(k, v_ref, uf_ref, xh_ref, xl_ref, wh_ref, wl_ref)
        backward(uf_ref, wh_ref, wl_ref)
        u_ref[1, 0:TARGETS, :], u_ref[1, TARGETS:, :] = split(uf_ref[...])
        across(4, u_ref.at[1], u_ref.at[1]).start()

    columns = []
    for step in range(2):
        if step == 1:

            @pl.when(core == 0)
            def _():
                across(3, u_ref.at[0], u_ref.at[0]).wait_send()
                across(4, u_ref.at[1], u_ref.at[1]).wait_recv()

            @pl.when(core == 1)
            def _():
                across(4, u_ref.at[1], u_ref.at[1]).wait_send()

        owned = (owner_ref[step] == me).astype(F32)
        before = pred_ref if step == 0 else new_pred_ref
        total = jnp.zeros((TARGETS, 1), F32)
        for start in range(0, ROWS, 256):
            cols = slice(start, start + 256)
            half = kernel_of(left_ref[step], right_ref[cols, :]).astype(BF16)
            new = before[:, cols] + mm(u_ref[step, 0:TARGETS, :], half)
            new_pred_ref[:, cols] = new
            placed = mm(u_ref[step], sel_ref[step, cols, :], NT)
            coef = new_coef_ref[:, cols] + owned * (placed[:TARGETS] + placed[TARGETS:])
            new_coef_ref[:, cols] = coef
            rest = residual_of(labels_ref[:, cols], new, coef)
            total = total + jnp.sum(rest * rest, axis=1, keepdims=True)
        columns.append(total)

    value = jnp.broadcast_to(jnp.concatenate(columns, axis=0), (128, 128)).T[0:8, :]
    groups = ((((1 - core, other),), core, got_c), (plane, place_at, got_p), (z_ring, z, got_z))
    for phase, (peers, at, slots) in enumerate(groups):
        slots[at] = value
        copies = []
        for position, device in peers:
            copy = pltpu.make_async_remote_copy(
                slots.at[at], slots.at[at], send_n.at[phase, position], recv_n.at[phase, at],
                device_id=(device,), device_id_type=MESH,
            )
            copy.start()
            copies.append(copy)
        for copy in copies:
            copy.wait_send()
        for position, device in peers:
            pltpu.make_async_remote_copy(
                slots.at[position], slots.at[position], send_n.at[phase, position],
                recv_n.at[phase, position], device_id=(device,), device_id_type=MESH,
            ).wait_recv()
        value = jnp.sum(slots[...], axis=0)
    sums_ref[...] = value


def finish_kernel(total_rows, pred_ref, coef_ref, sums_ref, out_pred_ref, out_coef_ref, out_ref):
    out_pred_ref[...] = pred_ref[...]
    out_coef_ref[...] = coef_ref[...]
    norms = jnp.sqrt(sums_ref[0:1, :] / total_rows + 1e-06)
    out_ref[0:1, :] = norms[:, 0:TARGETS]
    out_ref[1:2, :] = norms[:, TARGETS:]


def local(embeddings, labels, predictions, coefficients, block_index, owner_id):
    shape = jax.ShapeDtypeStruct
    total_rows = embeddings.shape[0] * lax.axis_size("rows")
    count = BLOCK // NB
    chips = NX * NY
    wide = shape((TARGETS, ROWS), F32)

    def room(*dims, kind=BF16):
        return pltpu.VMEM(dims, kind)

    new_pred, new_coef, sums = pl.pallas_call(
        descend_kernel,
        out_shape=[wide, wide, shape((8, 128), F32)],
        in_specs=[smem()] + [vmem()] * 5,
        out_specs=[vmem()] * 3,
        scratch_shapes=[
            room(2, 2, BLOCK, 128),
            room(2, BLOCK, 128),
            room(BLOCK, 128),
            room(BLOCK, 128),
            room(chips, BLOCK // chips, 128),
            room(NZ, BLOCK // chips, 128),
            room(chips, BLOCK // chips, 128),
            room(NZ, BLOCK // chips, 128),
            room(BLOCK, 128),
            room(BLOCK, 128),
            room(2, ROWS, BLOCK),
            room(ROWS, 2 * FEATURES),
            room(2, BLOCK, FEATURES),
            room(2, BLOCK, 2 * FEATURES),
            room(BLOCK, 2 * FEATURES),
            room(2, 2 * TARGETS, BLOCK),
            room(BLOCK, BLOCK, kind=F32),
            room(count, NB, NB),
            room(count, NB, NB),
            room(BLOCK, BLOCK),
            room(BLOCK, BLOCK),
            room(TARGETS, BLOCK, kind=F32),
            room(TARGETS, BLOCK, kind=F32),
            room(BLOCK, BLOCK),
            room(BLOCK, BLOCK),
            room(2, 8, 128, kind=F32),
            room(chips, 8, 128, kind=F32),
            room(NZ, 8, 128, kind=F32),
        ]
        + [pltpu.SemaphoreType.DMA((3, chips))] * 6
        + [pltpu.SemaphoreType.DMA((5,))] * 2,
        compiler_params=pltpu.CompilerParams(
            collective_id=0, has_side_effects=True, vmem_limit_bytes=VMEM_LIMIT
        ),
        name="descend",
    )(owner_id, embeddings, labels.reshape(1, ROWS), predictions, coefficients, block_index)

    return pl.pallas_call(
        functools.partial(finish_kernel, total_rows),
        out_shape=[wide, wide, shape((2, TARGETS), F32)],
        in_specs=[vmem()] * 3,
        out_specs=[vmem()] * 3,
        name="finish",
    )(new_pred, new_coef, sums)


def solution(mesh):
    in_specs = (P("rows", None), P("rows"), P(None, "rows"), P(None, "rows"), P(), P())
    out_specs = (P(None, "rows"), P(None, "rows"), P())
    return jax.shard_map(local, mesh=mesh, in_specs=in_specs, out_specs=out_specs, check_vma=False)
```

time: 83.1 us -> 73.5 us (0.88)
  Pallas kernels: 81 us -> 72.7 us
  local copies, waits for them, and re-layouts: 1.22 us -> 0 us
    pallas_call x3 -> x2, Pallas kernels: 81 us -> 72.7 us  [the longest x1 70.5 us: local(): pl.pallas_call(descend_kernel, out_shape=[wide, wide, shape((8, 128), F32...]
    unnamed x1 -> x0, local copies, waits for them, and re-layouts: 1.22 us -> none
where the time goes in v3:
time: 73.5 us; the launch traced here: 73.4 us
  Pallas kernels  72.7 us (99%)
    pallas_call x1, Pallas kernels, local(): pl.pallas_call(descend_kernel, out_shape=[wide, wide, shape((8, 128), F32...  70.5 us
    pallas_call x1, Pallas kernels, local(): pl.pallas_call(functools.partial(finish_kernel, total_rows), out_shape=[w...  2.2 us

profile of v3, /device:TPU:1, one launch (start us, length us, event | category | flops | bytes accessed | tf_op | source)
XLA Modules:
  0.0 73.4 jit_solution(11388468705068933024)
XLA Ops:
  0.6 70.5 %descend.1 = (f32[64,2048]{1,0:T(8,128)}, f32[64,2048]{1,0:T(8,128)}, f32[8,128]{1,0:T(8,128)}) custom-call(s32[2]{0:T(128)} %owner_ref.1, bf16[2048,128]{1,0:T(8,128)(2,1)} %rows_ref.1, s32[1,2048]{1,0:T(1,128)} %bitcast.1, f32[64,2048]{1,0:T(8,128)} %pred_ref.1, f32[64,2048]{1,0:T(8,128)} %coef_ref.1, s32[2,1024]{1,0:T(2,128)} %index_ref.1), custom_call_target="tpu_custom_call" | custom-call | tf_op jit(solution)/shard_map/descend/pallas_call | solution.py:437
  71.2 2.2 %finish.1 = (f32[64,2048]{1,0:T(8,128)}, f32[64,2048]{1,0:T(8,128)}, f32[2,64]{1,0:T(2,128)}) custom-call(f32[64,2048]{1,0:T(8,128)} %get-tuple-element.6.pred_ref, f32[64,2048]{1,0:T(8,128)} %get-tuple-element.7.coef_ref, f32[8,128]{1,0:T(8,128)} %get-tuple-element.8.sums_ref), custom_call_target="tpu_custom_call" | custom-call | tf_op jit(solution)/shard_map/finish/pallas_call | solution.py:480
